TPU v7x, 256 devices: a whole 4x4x8 slice. The times are simulated.
256 devices in a mesh: ka: 8 (over y_hi, x), band: 32 (over y_lo, z, core).
Axes of the slice: x: 4, y: 4 (y_hi: 2, y_lo: 2; y = y_hi * 2 + y_lo), z: 8, core: 2. Of those that a mesh axis runs over, the one named last changes fastest.
Arguments:
- targets: float32 [256, 2, 24, 576], P(('ka', 'band')), may hold values from -6 to 6
- occupied: bfloat16 [256, 2, 24, 576], P(('ka', 'band')), may hold values from -3 to 3
- kernels: float32 [16, 24, 576], replicated, may hold values from 0.1 to 2
- partner: int32 [8], replicated, may hold values from 0 to 7, as said below
- kernel_index: int32 [16, 16], replicated, may hold values from 0 to 15
Outputs:
- exchange: float32 [256, 2, 24, 576], P(('ka', 'band'))
Inputs may be any that keep to these rules, and one draw needn't show every extreme that they name: partner is a permutation of the groups.
All inputs are finite; a program needn't handle non-finite values.
Results may differ from a plain program's by a relative error of at most 0.0003.
Values may be sent and summed in bfloat16 or wider, within the bound.
A program may use at most 64 MiB of HBM per device.

v0:
```python
import jax
import jax.numpy as jnp
from jax import lax
from jax.sharding import PartitionSpec as P

GRID = 24
KPT_DEV = 2


def passed_along(array, axis, by):
    peers = lax.axis_size(axis)
    return lax.ppermute(array, axis, [(i, (i + by) % peers) for i in range(peers)])


def spectral_tables(grid_size):
    positions = jnp.arange(grid_size, dtype=jnp.int32)
    products = positions[:, None] * positions[None, :] % grid_size
    angles = products.astype(jnp.float32) * (2.0 * jnp.pi / grid_size)
    factor = 1.0 / jnp.sqrt(jnp.float32(grid_size))
    return (jnp.cos(angles) * factor, jnp.sin(angles) * factor)


def rotate_apply(source_field, matrix):
    batch_count, grid_size, plane_size = source_field.shape
    result = lax.dot_general(
        source_field,
        matrix,
        (((1,), (1,)), ((), ())),
        precision=lax.Precision.HIGHEST,
        preferred_element_type=jnp.float32,
    )
    return result.reshape(batch_count, grid_size, plane_size)


def transform(real_part, imag_part, cosine_table, sine_table, direction):
    for repeat in range(3):
        real_part, imag_part = (
            rotate_apply(real_part, cosine_table) - direction * rotate_apply(imag_part, sine_table),
            rotate_apply(imag_part, cosine_table) + direction * rotate_apply(real_part, sine_table),
        )
    return (real_part, imag_part)


def pair_term(orbital, target_real, target_imag, kernel, cosine_table, sine_table):
    orbital_values = orbital.astype(jnp.float32)
    orbital_real = orbital_values[0, 0]
    orbital_imag = orbital_values[0, 1]
    dens_real = orbital_real * target_real + orbital_imag * target_imag
    dens_imag = orbital_real * target_imag - orbital_imag * target_real
    spec_real, spec_imag = transform(dens_real, dens_imag, cosine_table, sine_table, -1.0)
    pot_real, pot_imag = transform(
        kernel * spec_real, kernel * spec_imag, cosine_table, sine_table, 1.0
    )
    return (
        orbital_real * pot_real - orbital_imag * pot_imag,
        orbital_real * pot_imag + orbital_imag * pot_real,
    )


def shards(targets, occupied, kernels, partner, kernel_index):
    band_count = lax.axis_size("band")
    per_kpoint = band_count // KPT_DEV
    my_group = lax.axis_index("ka")
    position = lax.axis_index("band")
    kpoint = my_group * KPT_DEV + position // per_kpoint
    cosine_table, sine_table = spectral_tables(GRID)
    target_real = targets[:, 0]
    target_imag = targets[:, 1]
    everyone = lax.all_gather(occupied, "ka", axis=0, tiled=True)
    partner_group = partner[my_group]
    visitor = lax.dynamic_slice_in_dim(everyone, partner_group, 1, 0)

    def contribute(totals, orbital, source_band):
        source_k = partner_group * KPT_DEV + source_band // per_kpoint
        table_row = kernel_index[kpoint, source_k]
        kernel = lax.dynamic_index_in_dim(kernels, table_row, 0, keepdims=False)
        more_real, more_imag = pair_term(
            orbital, target_real, target_imag, kernel, cosine_table, sine_table
        )
        return (totals[0] - more_real, totals[1] - more_imag)

    empty_field = jnp.zeros_like(target_real)
    totals = contribute((empty_field, empty_field), visitor, position)

    def onward(number, carried):
        current, summed = carried
        current = passed_along(current, "band", 1)
        return (current, contribute(summed, current, (position - number) % band_count))

    current, totals = lax.fori_loop(1, band_count, onward, (visitor, totals))
    return jnp.stack(totals, axis=1)


def solution(mesh):
    return jax.shard_map(
        shards,
        mesh=mesh,
        in_specs=(
            P(("ka", "band"), None, None, None),
            P(("ka", "band"), None, None, None),
            P(),
            P(),
            P(),
        ),
        out_specs=P(("ka", "band"), None, None, None),
        check_vma=False,
    )
```

profile of v0, /device:TPU:2, one launch (start us, length us, event | category | flops | bytes accessed | tf_op | source)
XLA Modules:
  0.0 548.9 jit_solution(14453901876114819552)
XLA Ops:
  6.8 35.1 %all_gather.3 = bf16[8,2,24,576]{3,2,1,0:T(8,128)(2,1)S(1)} all-gather(bf16[1,2,24,576]{3,2,1,0:T(8,128)(2,1)S(1)} %copy-done.2), channel_id=1, replica_groups=mesh['ka'=8,'band'=32] {'ka'}, dimensions={0}, use_global_device_ids=true | all-gather | bytes 497664 | tf_op jit(solution)/shard_map/all_gather | solution.py:69
  52.9 495.4 %while.21 = (s32[]{:T(128)}, bf16[1,2,24,576]{3,2,1,0:T(8,128)(2,1)S(1)}, f32[1,24,576]{2,1,0:T(8,128)S(1)}, f32[1,24,576]{2,1,0:T(8,128)S(1)}, s32[]{:T(128)}, ...) while((s32[]{:T(128)}, ...), condition=%wide.region_1.2_spmd.clone.clone, body=%wide.region_0.1_spmd.clone.clone.sunk | while | flops 96215040 | bytes 7526992 | solution.py:90
  56.4 2.5 collective-permute-done
  72.4 2.5 collective-permute-done
  88.4 2.5 collective-permute-done
  104.3 2.5 collective-permute-done
  120.3 2.5 collective-permute-done
  136.3 2.5 collective-permute-done
  152.3 2.5 collective-permute-done
  168.2 2.5 collective-permute-done
  184.2 2.5 collective-permute-done
  200.2 2.5 collective-permute-done
  216.2 2.5 collective-permute-done
  232.1 2.5 collective-permute-done
  248.1 2.5 collective-permute-done
  264.1 2.5 collective-permute-done
  280.1 2.5 collective-permute-done
  296.0 2.5 collective-permute-done
  312.0 2.5 collective-permute-done
  328.0 2.5 collective-permute-done
  344.0 2.5 collective-permute-done
  359.9 2.5 collective-permute-done
  375.9 2.5 collective-permute-done
  391.9 2.5 collective-permute-done
  407.9 2.5 collective-permute-done
  423.8 2.5 collective-permute-done
  439.8 2.5 collective-permute-done
  471.8 2.5 collective-permute-done
  487.7 2.5 collective-permute-done
  503.7 2.5 collective-permute-done
  519.7 2.5 collective-permute-done
  535.7 2.5 collective-permute-done
  (1735 shorter events, 362.3 us)
Async XLA Ops:
  0.0 6.8 %copy-start.2 = (bf16[1,2,24,576]{3,2,1,0:T(8,128)(2,1)S(1)}, bf16[1,2,24,576]{3,2,1,0:T(8,128)(2,1)}, u32[]{:S(2)}) copy-start(bf16[1,2,24,576]{3,2,1,0:T(8,128)(2,1)} %param.8) | copy-start | bytes 165892
  53.1 5.8 %collective-permute-start = (bf16[1,2,24,576]{3,2,1,0:T(8,128)(2,1)S(1)}, bf16[1,2,24,576]{3,2,1,0:T(8,128)(2,1)S(1)}, u32[]{:S(2)}, u32[]{:S(2)}) collective-permute-start(bf16[1,2,24,576]{3,2,1,0:T(8,128)(2,1)S(1)} %get-tuple-element.598), channel_id=1, source_target_pairs={{0,1},{1,2},{2,3},{3,4},{4,5},{5,6},{6,7},{7,8},{8,9},{9,10},{10,1... | collective-permute-start | bytes 165896 | tf_op jit(solution)/shard_map/while/body/eval_jaxpr/ppermute | solution.py:12
  69.0 5.8 %collective-permute-start = (bf16[1,2,24,576]{3,2,1,0:T(8,128)(2,1)S(1)}, bf16[1,2,24,576]{3,2,1,0:T(8,128)(2,1)S(1)}, u32[]{:S(2)}, u32[]{:S(2)}) collective-permute-start(bf16[1,2,24,576]{3,2,1,0:T(8,128)(2,1)S(1)} %get-tuple-element.598), channel_id=1, source_target_pairs={{0,1},{1,2},{2,3},{3,4},{4,5},{5,6},{6,7},{7,8},{8,9},{9,10},{10,1... | collective-permute-start | bytes 165896 | tf_op jit(solution)/shard_map/while/body/eval_jaxpr/ppermute | solution.py:12
  85.0 5.8 %collective-permute-start = (bf16[1,2,24,576]{3,2,1,0:T(8,128)(2,1)S(1)}, bf16[1,2,24,576]{3,2,1,0:T(8,128)(2,1)S(1)}, u32[]{:S(2)}, u32[]{:S(2)}) collective-permute-start(bf16[1,2,24,576]{3,2,1,0:T(8,128)(2,1)S(1)} %get-tuple-element.598), channel_id=1, source_target_pairs={{0,1},{1,2},{2,3},{3,4},{4,5},{5,6},{6,7},{7,8},{8,9},{9,10},{10,1... | collective-permute-start | bytes 165896 | tf_op jit(solution)/shard_map/while/body/eval_jaxpr/ppermute | solution.py:12
  101.0 5.8 %collective-permute-start = (bf16[1,2,24,576]{3,2,1,0:T(8,128)(2,1)S(1)}, bf16[1,2,24,576]{3,2,1,0:T(8,128)(2,1)S(1)}, u32[]{:S(2)}, u32[]{:S(2)}) collective-permute-start(bf16[1,2,24,576]{3,2,1,0:T(8,128)(2,1)S(1)} %get-tuple-element.598), channel_id=1, source_target_pairs={{0,1},{1,2},{2,3},{3,4},{4,5},{5,6},{6,7},{7,8},{8,9},{9,10},{10,1... | collective-permute-start | bytes 165896 | tf_op jit(solution)/shard_map/while/body/eval_jaxpr/ppermute | solution.py:12
  117.0 5.8 %collective-permute-start = (bf16[1,2,24,576]{3,2,1,0:T(8,128)(2,1)S(1)}, bf16[1,2,24,576]{3,2,1,0:T(8,128)(2,1)S(1)}, u32[]{:S(2)}, u32[]{:S(2)}) collective-permute-start(bf16[1,2,24,576]{3,2,1,0:T(8,128)(2,1)S(1)} %get-tuple-element.598), channel_id=1, source_target_pairs={{0,1},{1,2},{2,3},{3,4},{4,5},{5,6},{6,7},{7,8},{8,9},{9,10},{10,1... | collective-permute-start | bytes 165896 | tf_op jit(solution)/shard_map/while/body/eval_jaxpr/ppermute | solution.py:12
  132.9 5.8 %collective-permute-start = (bf16[1,2,24,576]{3,2,1,0:T(8,128)(2,1)S(1)}, bf16[1,2,24,576]{3,2,1,0:T(8,128)(2,1)S(1)}, u32[]{:S(2)}, u32[]{:S(2)}) collective-permute-start(bf16[1,2,24,576]{3,2,1,0:T(8,128)(2,1)S(1)} %get-tuple-element.598), channel_id=1, source_target_pairs={{0,1},{1,2},{2,3},{3,4},{4,5},{5,6},{6,7},{7,8},{8,9},{9,10},{10,1... | collective-permute-start | bytes 165896 | tf_op jit(solution)/shard_map/while/body/eval_jaxpr/ppermute | solution.py:12
  148.9 5.8 %collective-permute-start = (bf16[1,2,24,576]{3,2,1,0:T(8,128)(2,1)S(1)}, bf16[1,2,24,576]{3,2,1,0:T(8,128)(2,1)S(1)}, u32[]{:S(2)}, u32[]{:S(2)}) collective-permute-start(bf16[1,2,24,576]{3,2,1,0:T(8,128)(2,1)S(1)} %get-tuple-element.598), channel_id=1, source_target_pairs={{0,1},{1,2},{2,3},{3,4},{4,5},{5,6},{6,7},{7,8},{8,9},{9,10},{10,1... | collective-permute-start | bytes 165896 | tf_op jit(solution)/shard_map/while/body/eval_jaxpr/ppermute | solution.py:12
  164.9 5.8 %collective-permute-start = (bf16[1,2,24,576]{3,2,1,0:T(8,128)(2,1)S(1)}, bf16[1,2,24,576]{3,2,1,0:T(8,128)(2,1)S(1)}, u32[]{:S(2)}, u32[]{:S(2)}) collective-permute-start(bf16[1,2,24,576]{3,2,1,0:T(8,128)(2,1)S(1)} %get-tuple-element.598), channel_id=1, source_target_pairs={{0,1},{1,2},{2,3},{3,4},{4,5},{5,6},{6,7},{7,8},{8,9},{9,10},{10,1... | collective-permute-start | bytes 165896 | tf_op jit(solution)/shard_map/while/body/eval_jaxpr/ppermute | solution.py:12
  180.9 5.8 %collective-permute-start = (bf16[1,2,24,576]{3,2,1,0:T(8,128)(2,1)S(1)}, bf16[1,2,24,576]{3,2,1,0:T(8,128)(2,1)S(1)}, u32[]{:S(2)}, u32[]{:S(2)}) collective-permute-start(bf16[1,2,24,576]{3,2,1,0:T(8,128)(2,1)S(1)} %get-tuple-element.598), channel_id=1, source_target_pairs={{0,1},{1,2},{2,3},{3,4},{4,5},{5,6},{6,7},{7,8},{8,9},{9,10},{10,1... | collective-permute-start | bytes 165896 | tf_op jit(solution)/shard_map/while/body/eval_jaxpr/ppermute | solution.py:12
  196.8 5.8 %collective-permute-start = (bf16[1,2,24,576]{3,2,1,0:T(8,128)(2,1)S(1)}, bf16[1,2,24,576]{3,2,1,0:T(8,128)(2,1)S(1)}, u32[]{:S(2)}, u32[]{:S(2)}) collective-permute-start(bf16[1,2,24,576]{3,2,1,0:T(8,128)(2,1)S(1)} %get-tuple-element.598), channel_id=1, source_target_pairs={{0,1},{1,2},{2,3},{3,4},{4,5},{5,6},{6,7},{7,8},{8,9},{9,10},{10,1... | collective-permute-start | bytes 165896 | tf_op jit(solution)/shard_map/while/body/eval_jaxpr/ppermute | solution.py:12
  212.8 5.8 %collective-permute-start = (bf16[1,2,24,576]{3,2,1,0:T(8,128)(2,1)S(1)}, bf16[1,2,24,576]{3,2,1,0:T(8,128)(2,1)S(1)}, u32[]{:S(2)}, u32[]{:S(2)}) collective-permute-start(bf16[1,2,24,576]{3,2,1,0:T(8,128)(2,1)S(1)} %get-tuple-element.598), channel_id=1, source_target_pairs={{0,1},{1,2},{2,3},{3,4},{4,5},{5,6},{6,7},{7,8},{8,9},{9,10},{10,1... | collective-permute-start | bytes 165896 | tf_op jit(solution)/shard_map/while/body/eval_jaxpr/ppermute | solution.py:12
  228.8 5.8 %collective-permute-start = (bf16[1,2,24,576]{3,2,1,0:T(8,128)(2,1)S(1)}, bf16[1,2,24,576]{3,2,1,0:T(8,128)(2,1)S(1)}, u32[]{:S(2)}, u32[]{:S(2)}) collective-permute-start(bf16[1,2,24,576]{3,2,1,0:T(8,128)(2,1)S(1)} %get-tuple-element.598), channel_id=1, source_target_pairs={{0,1},{1,2},{2,3},{3,4},{4,5},{5,6},{6,7},{7,8},{8,9},{9,10},{10,1... | collective-permute-start | bytes 165896 | tf_op jit(solution)/shard_map/while/body/eval_jaxpr/ppermute | solution.py:12
  244.8 5.8 %collective-permute-start = (bf16[1,2,24,576]{3,2,1,0:T(8,128)(2,1)S(1)}, bf16[1,2,24,576]{3,2,1,0:T(8,128)(2,1)S(1)}, u32[]{:S(2)}, u32[]{:S(2)}) collective-permute-start(bf16[1,2,24,576]{3,2,1,0:T(8,128)(2,1)S(1)} %get-tuple-element.598), channel_id=1, source_target_pairs={{0,1},{1,2},{2,3},{3,4},{4,5},{5,6},{6,7},{7,8},{8,9},{9,10},{10,1... | collective-permute-start | bytes 165896 | tf_op jit(solution)/shard_map/while/body/eval_jaxpr/ppermute | solution.py:12
  260.7 5.8 %collective-permute-start = (bf16[1,2,24,576]{3,2,1,0:T(8,128)(2,1)S(1)}, bf16[1,2,24,576]{3,2,1,0:T(8,128)(2,1)S(1)}, u32[]{:S(2)}, u32[]{:S(2)}) collective-permute-start(bf16[1,2,24,576]{3,2,1,0:T(8,128)(2,1)S(1)} %get-tuple-element.598), channel_id=1, source_target_pairs={{0,1},{1,2},{2,3},{3,4},{4,5},{5,6},{6,7},{7,8},{8,9},{9,10},{10,1... | collective-permute-start | bytes 165896 | tf_op jit(solution)/shard_map/while/body/eval_jaxpr/ppermute | solution.py:12
  276.7 5.8 %collective-permute-start = (bf16[1,2,24,576]{3,2,1,0:T(8,128)(2,1)S(1)}, bf16[1,2,24,576]{3,2,1,0:T(8,128)(2,1)S(1)}, u32[]{:S(2)}, u32[]{:S(2)}) collective-permute-start(bf16[1,2,24,576]{3,2,1,0:T(8,128)(2,1)S(1)} %get-tuple-element.598), channel_id=1, source_target_pairs={{0,1},{1,2},{2,3},{3,4},{4,5},{5,6},{6,7},{7,8},{8,9},{9,10},{10,1... | collective-permute-start | bytes 165896 | tf_op jit(solution)/shard_map/while/body/eval_jaxpr/ppermute | solution.py:12
  292.7 5.8 %collective-permute-start = (bf16[1,2,24,576]{3,2,1,0:T(8,128)(2,1)S(1)}, bf16[1,2,24,576]{3,2,1,0:T(8,128)(2,1)S(1)}, u32[]{:S(2)}, u32[]{:S(2)}) collective-permute-start(bf16[1,2,24,576]{3,2,1,0:T(8,128)(2,1)S(1)} %get-tuple-element.598), channel_id=1, source_target_pairs={{0,1},{1,2},{2,3},{3,4},{4,5},{5,6},{6,7},{7,8},{8,9},{9,10},{10,1... | collective-permute-start | bytes 165896 | tf_op jit(solution)/shard_map/while/body/eval_jaxpr/ppermute | solution.py:12
  308.7 5.8 %collective-permute-start = (bf16[1,2,24,576]{3,2,1,0:T(8,128)(2,1)S(1)}, bf16[1,2,24,576]{3,2,1,0:T(8,128)(2,1)S(1)}, u32[]{:S(2)}, u32[]{:S(2)}) collective-permute-start(bf16[1,2,24,576]{3,2,1,0:T(8,128)(2,1)S(1)} %get-tuple-element.598), channel_id=1, source_target_pairs={{0,1},{1,2},{2,3},{3,4},{4,5},{5,6},{6,7},{7,8},{8,9},{9,10},{10,1... | collective-permute-start | bytes 165896 | tf_op jit(solution)/shard_map/while/body/eval_jaxpr/ppermute | solution.py:12
  324.6 5.8 %collective-permute-start = (bf16[1,2,24,576]{3,2,1,0:T(8,128)(2,1)S(1)}, bf16[1,2,24,576]{3,2,1,0:T(8,128)(2,1)S(1)}, u32[]{:S(2)}, u32[]{:S(2)}) collective-permute-start(bf16[1,2,24,576]{3,2,1,0:T(8,128)(2,1)S(1)} %get-tuple-element.598), channel_id=1, source_target_pairs={{0,1},{1,2},{2,3},{3,4},{4,5},{5,6},{6,7},{7,8},{8,9},{9,10},{10,1... | collective-permute-start | bytes 165896 | tf_op jit(solution)/shard_map/while/body/eval_jaxpr/ppermute | solution.py:12
  340.6 5.8 %collective-permute-start = (bf16[1,2,24,576]{3,2,1,0:T(8,128)(2,1)S(1)}, bf16[1,2,24,576]{3,2,1,0:T(8,128)(2,1)S(1)}, u32[]{:S(2)}, u32[]{:S(2)}) collective-permute-start(bf16[1,2,24,576]{3,2,1,0:T(8,128)(2,1)S(1)} %get-tuple-element.598), channel_id=1, source_target_pairs={{0,1},{1,2},{2,3},{3,4},{4,5},{5,6},{6,7},{7,8},{8,9},{9,10},{10,1... | collective-permute-start | bytes 165896 | tf_op jit(solution)/shard_map/while/body/eval_jaxpr/ppermute | solution.py:12
  356.6 5.8 %collective-permute-start = (bf16[1,2,24,576]{3,2,1,0:T(8,128)(2,1)S(1)}, bf16[1,2,24,576]{3,2,1,0:T(8,128)(2,1)S(1)}, u32[]{:S(2)}, u32[]{:S(2)}) collective-permute-start(bf16[1,2,24,576]{3,2,1,0:T(8,128)(2,1)S(1)} %get-tuple-element.598), channel_id=1, source_target_pairs={{0,1},{1,2},{2,3},{3,4},{4,5},{5,6},{6,7},{7,8},{8,9},{9,10},{10,1... | collective-permute-start | bytes 165896 | tf_op jit(solution)/shard_map/while/body/eval_jaxpr/ppermute | solution.py:12
  372.6 5.8 %collective-permute-start = (bf16[1,2,24,576]{3,2,1,0:T(8,128)(2,1)S(1)}, bf16[1,2,24,576]{3,2,1,0:T(8,128)(2,1)S(1)}, u32[]{:S(2)}, u32[]{:S(2)}) collective-permute-start(bf16[1,2,24,576]{3,2,1,0:T(8,128)(2,1)S(1)} %get-tuple-element.598), channel_id=1, source_target_pairs={{0,1},{1,2},{2,3},{3,4},{4,5},{5,6},{6,7},{7,8},{8,9},{9,10},{10,1... | collective-permute-start | bytes 165896 | tf_op jit(solution)/shard_map/while/body/eval_jaxpr/ppermute | solution.py:12
  388.5 5.8 %collective-permute-start = (bf16[1,2,24,576]{3,2,1,0:T(8,128)(2,1)S(1)}, bf16[1,2,24,576]{3,2,1,0:T(8,128)(2,1)S(1)}, u32[]{:S(2)}, u32[]{:S(2)}) collective-permute-start(bf16[1,2,24,576]{3,2,1,0:T(8,128)(2,1)S(1)} %get-tuple-element.598), channel_id=1, source_target_pairs={{0,1},{1,2},{2,3},{3,4},{4,5},{5,6},{6,7},{7,8},{8,9},{9,10},{10,1... | collective-permute-start | bytes 165896 | tf_op jit(solution)/shard_map/while/body/eval_jaxpr/ppermute | solution.py:12
  404.5 5.8 %collective-permute-start = (bf16[1,2,24,576]{3,2,1,0:T(8,128)(2,1)S(1)}, bf16[1,2,24,576]{3,2,1,0:T(8,128)(2,1)S(1)}, u32[]{:S(2)}, u32[]{:S(2)}) collective-permute-start(bf16[1,2,24,576]{3,2,1,0:T(8,128)(2,1)S(1)} %get-tuple-element.598), channel_id=1, source_target_pairs={{0,1},{1,2},{2,3},{3,4},{4,5},{5,6},{6,7},{7,8},{8,9},{9,10},{10,1... | collective-permute-start | bytes 165896 | tf_op jit(solution)/shard_map/while/body/eval_jaxpr/ppermute | solution.py:12
  420.5 5.8 %collective-permute-start = (bf16[1,2,24,576]{3,2,1,0:T(8,128)(2,1)S(1)}, bf16[1,2,24,576]{3,2,1,0:T(8,128)(2,1)S(1)}, u32[]{:S(2)}, u32[]{:S(2)}) collective-permute-start(bf16[1,2,24,576]{3,2,1,0:T(8,128)(2,1)S(1)} %get-tuple-element.598), channel_id=1, source_target_pairs={{0,1},{1,2},{2,3},{3,4},{4,5},{5,6},{6,7},{7,8},{8,9},{9,10},{10,1... | collective-permute-start | bytes 165896 | tf_op jit(solution)/shard_map/while/body/eval_jaxpr/ppermute | solution.py:12
  436.5 5.8 %collective-permute-start = (bf16[1,2,24,576]{3,2,1,0:T(8,128)(2,1)S(1)}, bf16[1,2,24,576]{3,2,1,0:T(8,128)(2,1)S(1)}, u32[]{:S(2)}, u32[]{:S(2)}) collective-permute-start(bf16[1,2,24,576]{3,2,1,0:T(8,128)(2,1)S(1)} %get-tuple-element.598), channel_id=1, source_target_pairs={{0,1},{1,2},{2,3},{3,4},{4,5},{5,6},{6,7},{7,8},{8,9},{9,10},{10,1... | collective-permute-start | bytes 165896 | tf_op jit(solution)/shard_map/while/body/eval_jaxpr/ppermute | solution.py:12
  452.4 5.8 %collective-permute-start = (bf16[1,2,24,576]{3,2,1,0:T(8,128)(2,1)S(1)}, bf16[1,2,24,576]{3,2,1,0:T(8,128)(2,1)S(1)}, u32[]{:S(2)}, u32[]{:S(2)}) collective-permute-start(bf16[1,2,24,576]{3,2,1,0:T(8,128)(2,1)S(1)} %get-tuple-element.598), channel_id=1, source_target_pairs={{0,1},{1,2},{2,3},{3,4},{4,5},{5,6},{6,7},{7,8},{8,9},{9,10},{10,1... | collective-permute-start | bytes 165896 | tf_op jit(solution)/shard_map/while/body/eval_jaxpr/ppermute | solution.py:12
  468.4 5.8 %collective-permute-start = (bf16[1,2,24,576]{3,2,1,0:T(8,128)(2,1)S(1)}, bf16[1,2,24,576]{3,2,1,0:T(8,128)(2,1)S(1)}, u32[]{:S(2)}, u32[]{:S(2)}) collective-permute-start(bf16[1,2,24,576]{3,2,1,0:T(8,128)(2,1)S(1)} %get-tuple-element.598), channel_id=1, source_target_pairs={{0,1},{1,2},{2,3},{3,4},{4,5},{5,6},{6,7},{7,8},{8,9},{9,10},{10,1... | collective-permute-start | bytes 165896 | tf_op jit(solution)/shard_map/while/body/eval_jaxpr/ppermute | solution.py:12
  484.4 5.8 %collective-permute-start = (bf16[1,2,24,576]{3,2,1,0:T(8,128)(2,1)S(1)}, bf16[1,2,24,576]{3,2,1,0:T(8,128)(2,1)S(1)}, u32[]{:S(2)}, u32[]{:S(2)}) collective-permute-start(bf16[1,2,24,576]{3,2,1,0:T(8,128)(2,1)S(1)} %get-tuple-element.598), channel_id=1, source_target_pairs={{0,1},{1,2},{2,3},{3,4},{4,5},{5,6},{6,7},{7,8},{8,9},{9,10},{10,1... | collective-permute-start | bytes 165896 | tf_op jit(solution)/shard_map/while/body/eval_jaxpr/ppermute | solution.py:12
  500.4 5.8 %collective-permute-start = (bf16[1,2,24,576]{3,2,1,0:T(8,128)(2,1)S(1)}, bf16[1,2,24,576]{3,2,1,0:T(8,128)(2,1)S(1)}, u32[]{:S(2)}, u32[]{:S(2)}) collective-permute-start(bf16[1,2,24,576]{3,2,1,0:T(8,128)(2,1)S(1)} %get-tuple-element.598), channel_id=1, source_target_pairs={{0,1},{1,2},{2,3},{3,4},{4,5},{5,6},{6,7},{7,8},{8,9},{9,10},{10,1... | collective-permute-start | bytes 165896 | tf_op jit(solution)/shard_map/while/body/eval_jaxpr/ppermute | solution.py:12
  516.3 5.8 %collective-permute-start = (bf16[1,2,24,576]{3,2,1,0:T(8,128)(2,1)S(1)}, bf16[1,2,24,576]{3,2,1,0:T(8,128)(2,1)S(1)}, u32[]{:S(2)}, u32[]{:S(2)}) collective-permute-start(bf16[1,2,24,576]{3,2,1,0:T(8,128)(2,1)S(1)} %get-tuple-element.598), channel_id=1, source_target_pairs={{0,1},{1,2},{2,3},{3,4},{4,5},{5,6},{6,7},{7,8},{8,9},{9,10},{10,1... | collective-permute-start | bytes 165896 | tf_op jit(solution)/shard_map/while/body/eval_jaxpr/ppermute | solution.py:12
  532.3 5.8 %collective-permute-start = (bf16[1,2,24,576]{3,2,1,0:T(8,128)(2,1)S(1)}, bf16[1,2,24,576]{3,2,1,0:T(8,128)(2,1)S(1)}, u32[]{:S(2)}, u32[]{:S(2)}) collective-permute-start(bf16[1,2,24,576]{3,2,1,0:T(8,128)(2,1)S(1)} %get-tuple-element.598), channel_id=1, source_target_pairs={{0,1},{1,2},{2,3},{3,4},{4,5},{5,6},{6,7},{7,8},{8,9},{9,10},{10,1... | collective-permute-start | bytes 165896 | tf_op jit(solution)/shard_map/while/body/eval_jaxpr/ppermute | solution.py:12
  (2 other events, 2.3 us)
where the time goes:
time: 551 us; the launch traced here: 549 us
  matrix products  200 us (36%)
  local copies, waits for them, and re-layouts  154 us (28%)
  waiting for transfers between devices  77 us (14%)
  loops' own time  72.5 us (13%)
  blocking collectives  35.1 us (6%)
    dot_general x768, matrix products, rotate_apply(): lax.dot_general(source_field, matrix, (((1,), (1,)), ((), ())), precision...  200 us
    ppermute x31, waiting for transfers between devices, passed_along(): lax.ppermute(array, axis, [(i, (i + by) % peers) for i in range(peers)])  77 us
    another operation x1, loops' own time, shards(): current, totals = lax.fori_loop(1, band_count, onward, (visitor, totals))  72.5 us
    sub x384, local copies, waits for them, and re-layouts, transform(): rotate_apply(real_part, cosine_table)  55.1 us
    add x384, local copies, waits for them, and re-layouts, transform(): rotate_apply(imag_part, cosine_table)  55.1 us
    dynamic_slice x32, local copies, waits for them, and re-layouts, contribute(): table_row = kernel_index[kpoint, source_k]  41.6 us
    all_gather x1, blocking collectives, shards(): everyone = lax.all_gather(occupied, 'ka', axis=0, tiled=True)  35.1 us
  transfers between devices with their start and end apart: 31, of which 31 were waited for; matrix products, arithmetic and copies ran while one was open for 7% of the time, Pallas kernels for 0%

commit v1 on v0

--- a/solution.py
+++ b/solution.py
@@ -5,6 +5,16 @@
 
 GRID = 24
 KPT_DEV = 2
+
+
+def works_take(here_x):
+    pile = []
+    for _ in range(lax.psum(1, "ka")):
+        pile.append(here_x)
+    shaped = jnp.concatenate(
+        lax.all_to_all(jnp.stack(pile), axis_name="ka", split_axis=0, concat_axis=0), axis=0
+    )
+    return shaped
 
 
 def passed_along(array, axis, by):
@@ -66,7 +76,7 @@
     cosine_table, sine_table = spectral_tables(GRID)
     target_real = targets[:, 0]
     target_imag = targets[:, 1]
-    everyone = lax.all_gather(occupied, "ka", axis=0, tiled=True)
+    everyone = works_take(occupied)
     partner_group = partner[my_group]
     visitor = lax.dynamic_slice_in_dim(everyone, partner_group, 1, 0)
 

time: 551 us -> 529 us (0.960)
  blocking collectives: 35.1 us -> 0 us
  starting transfers between devices: 2.58 us -> 10 us
    all_gather x1 -> x0, blocking collectives: 35.1 us -> none  [shards(): everyone = lax.all_gather(occupied, 'ka', axis=0, tiled=True)]
    all_to_all x0 -> x1, starting transfers between devices: none -> 7.46 us  [works_take(): lax.all_to_all(jnp.stack(pile), axis_name='ka', split_axis=0, concat_axis=0)]
  transfers between devices with their start and end apart: 31 -> 32, of which waited for: 31 -> 32; matrix products, arithmetic and copies ran while one was open for 7% -> 8% of each run, Pallas kernels for 0% -> 0%
where the time goes in v1:
time: 529 us; the launch traced here: 526 us
  matrix products  200 us (38%)
  local copies, waits for them, and re-layouts  156 us (29%)
  waiting for transfers between devices  80.3 us (15%)
  loops' own time  71.2 us (13%)
  starting transfers between devices  10 us (2%)
    dot_general x768, matrix products, rotate_apply(): lax.dot_general(source_field, matrix, (((1,), (1,)), ((), ())), precision...  200 us
    ppermute x31, waiting for transfers between devices, passed_along(): lax.ppermute(array, axis, [(i, (i + by) % peers) for i in range(peers)])  77.3 us
    another operation x1, loops' own time, shards(): current, totals = lax.fori_loop(1, band_count, onward, (visitor, totals))  71.2 us
    add x384, local copies, waits for them, and re-layouts, transform(): rotate_apply(imag_part, cosine_table)  55.1 us
    sub x384, local copies, waits for them, and re-layouts, transform(): rotate_apply(real_part, cosine_table)  55.1 us
    dynamic_slice x32, local copies, waits for them, and re-layouts, contribute(): table_row = kernel_index[kpoint, source_k]  42.9 us
  transfers between devices with their start and end apart: 32, of which 32 were waited for; matrix products, arithmetic and copies ran while one was open for 8% of the time, Pallas kernels for 0%

profile of v1, /device:TPU:2, one launch (start us, length us, event | category | flops | bytes accessed | tf_op | source)
XLA Modules:
  0.0 525.6 jit_solution(11325345018465727485)
XLA Ops:
  1.7 7.5 %all-to-all-start = ((bf16[8,1,2,24,576]{4,3,2,1,0:T(8,128)(2,1)}), bf16[8,1,2,24,576]{4,3,2,1,0:T(8,128)(2,1)S(1)}, u32[]{:S(2)}, u32[]{:S(2)}) async-start(bf16[8,1,2,24,576]{4,3,2,1,0:T(8,128)(2,1)} %stack.8), calls=%async_computation | async-start | bytes 983040 | tf_op jit(solution)/shard_map/all_to_all | solution.py:15
  16.2 2.9 all-to-all-done
  29.3 495.6 %while.21 = (s32[]{:T(128)}, bf16[1,2,24,576]{3,2,1,0:T(8,128)(2,1)S(1)}, f32[1,24,576]{2,1,0:T(8,128)S(1)}, f32[1,24,576]{2,1,0:T(8,128)S(1)}, s32[]{:T(128)}, ...) while((s32[]{:T(128)}, ...), condition=%wide.region_1.2_spmd.clone.clone, body=%wide.region_0.1_spmd.clone.clone.sunk | while | flops 96215040 | bytes 7526992 | solution.py:100
  32.9 2.8 collective-permute-done
  49.2 2.5 collective-permute-done
  65.1 2.5 collective-permute-done
  81.1 2.5 collective-permute-done
  97.1 2.5 collective-permute-done
  113.0 2.5 collective-permute-done
  129.0 2.5 collective-permute-done
  145.0 2.5 collective-permute-done
  161.0 2.5 collective-permute-done
  176.9 2.5 collective-permute-done
  192.9 2.5 collective-permute-done
  208.9 2.5 collective-permute-done
  224.8 2.5 collective-permute-done
  240.8 2.5 collective-permute-done
  256.8 2.5 collective-permute-done
  272.7 2.5 collective-permute-done
  288.7 2.5 collective-permute-done
  304.7 2.5 collective-permute-done
  320.7 2.5 collective-permute-done
  336.6 2.5 collective-permute-done
  352.6 2.5 collective-permute-done
  368.6 2.5 collective-permute-done
  384.5 2.5 collective-permute-done
  400.5 2.5 collective-permute-done
  416.5 2.5 collective-permute-done
  432.5 2.5 collective-permute-done
  448.4 2.5 collective-permute-done
  464.4 2.5 collective-permute-done
  480.4 2.5 collective-permute-done
  (1737 shorter events, 366.7 us)
Async XLA Ops:
  1.7 17.5 %all-to-all-start = ((bf16[8,1,2,24,576]{4,3,2,1,0:T(8,128)(2,1)}), bf16[8,1,2,24,576]{4,3,2,1,0:T(8,128)(2,1)S(1)}, u32[]{:S(2)}, u32[]{:S(2)}) async-start(bf16[8,1,2,24,576]{4,3,2,1,0:T(8,128)(2,1)} %stack.8), calls=%async_computation | async-start | bytes 983040 | tf_op jit(solution)/shard_map/all_to_all | solution.py:15
  29.5 6.2 %collective-permute-start = (bf16[1,2,24,576]{3,2,1,0:T(8,128)(2,1)S(1)}, bf16[1,2,24,576]{3,2,1,0:T(8,128)(2,1)S(1)}, u32[]{:S(2)}, u32[]{:S(2)}) collective-permute-start(bf16[1,2,24,576]{3,2,1,0:T(8,128)(2,1)S(1)} %get-tuple-element.598), channel_id=1, source_target_pairs={{0,1},{1,2},{2,3},{3,4},{4,5},{5,6},{6,7},{7,8},{8,9},{9,10},{10,1... | collective-permute-start | bytes 165896 | tf_op jit(solution)/shard_map/while/body/eval_jaxpr/ppermute | solution.py:22
  45.8 5.8 %collective-permute-start = (bf16[1,2,24,576]{3,2,1,0:T(8,128)(2,1)S(1)}, bf16[1,2,24,576]{3,2,1,0:T(8,128)(2,1)S(1)}, u32[]{:S(2)}, u32[]{:S(2)}) collective-permute-start(bf16[1,2,24,576]{3,2,1,0:T(8,128)(2,1)S(1)} %get-tuple-element.598), channel_id=1, source_target_pairs={{0,1},{1,2},{2,3},{3,4},{4,5},{5,6},{6,7},{7,8},{8,9},{9,10},{10,1... | collective-permute-start | bytes 165896 | tf_op jit(solution)/shard_map/while/body/eval_jaxpr/ppermute | solution.py:22
  61.8 5.8 %collective-permute-start = (bf16[1,2,24,576]{3,2,1,0:T(8,128)(2,1)S(1)}, bf16[1,2,24,576]{3,2,1,0:T(8,128)(2,1)S(1)}, u32[]{:S(2)}, u32[]{:S(2)}) collective-permute-start(bf16[1,2,24,576]{3,2,1,0:T(8,128)(2,1)S(1)} %get-tuple-element.598), channel_id=1, source_target_pairs={{0,1},{1,2},{2,3},{3,4},{4,5},{5,6},{6,7},{7,8},{8,9},{9,10},{10,1... | collective-permute-start | bytes 165896 | tf_op jit(solution)/shard_map/while/body/eval_jaxpr/ppermute | solution.py:22
  77.7 5.8 %collective-permute-start = (bf16[1,2,24,576]{3,2,1,0:T(8,128)(2,1)S(1)}, bf16[1,2,24,576]{3,2,1,0:T(8,128)(2,1)S(1)}, u32[]{:S(2)}, u32[]{:S(2)}) collective-permute-start(bf16[1,2,24,576]{3,2,1,0:T(8,128)(2,1)S(1)} %get-tuple-element.598), channel_id=1, source_target_pairs={{0,1},{1,2},{2,3},{3,4},{4,5},{5,6},{6,7},{7,8},{8,9},{9,10},{10,1... | collective-permute-start | bytes 165896 | tf_op jit(solution)/shard_map/while/body/eval_jaxpr/ppermute | solution.py:22
  93.7 5.8 %collective-permute-start = (bf16[1,2,24,576]{3,2,1,0:T(8,128)(2,1)S(1)}, bf16[1,2,24,576]{3,2,1,0:T(8,128)(2,1)S(1)}, u32[]{:S(2)}, u32[]{:S(2)}) collective-permute-start(bf16[1,2,24,576]{3,2,1,0:T(8,128)(2,1)S(1)} %get-tuple-element.598), channel_id=1, source_target_pairs={{0,1},{1,2},{2,3},{3,4},{4,5},{5,6},{6,7},{7,8},{8,9},{9,10},{10,1... | collective-permute-start | bytes 165896 | tf_op jit(solution)/shard_map/while/body/eval_jaxpr/ppermute | solution.py:22
  109.7 5.8 %collective-permute-start = (bf16[1,2,24,576]{3,2,1,0:T(8,128)(2,1)S(1)}, bf16[1,2,24,576]{3,2,1,0:T(8,128)(2,1)S(1)}, u32[]{:S(2)}, u32[]{:S(2)}) collective-permute-start(bf16[1,2,24,576]{3,2,1,0:T(8,128)(2,1)S(1)} %get-tuple-element.598), channel_id=1, source_target_pairs={{0,1},{1,2},{2,3},{3,4},{4,5},{5,6},{6,7},{7,8},{8,9},{9,10},{10,1... | collective-permute-start | bytes 165896 | tf_op jit(solution)/shard_map/while/body/eval_jaxpr/ppermute | solution.py:22
  125.7 5.8 %collective-permute-start = (bf16[1,2,24,576]{3,2,1,0:T(8,128)(2,1)S(1)}, bf16[1,2,24,576]{3,2,1,0:T(8,128)(2,1)S(1)}, u32[]{:S(2)}, u32[]{:S(2)}) collective-permute-start(bf16[1,2,24,576]{3,2,1,0:T(8,128)(2,1)S(1)} %get-tuple-element.598), channel_id=1, source_target_pairs={{0,1},{1,2},{2,3},{3,4},{4,5},{5,6},{6,7},{7,8},{8,9},{9,10},{10,1... | collective-permute-start | bytes 165896 | tf_op jit(solution)/shard_map/while/body/eval_jaxpr/ppermute | solution.py:22
  141.6 5.8 %collective-permute-start = (bf16[1,2,24,576]{3,2,1,0:T(8,128)(2,1)S(1)}, bf16[1,2,24,576]{3,2,1,0:T(8,128)(2,1)S(1)}, u32[]{:S(2)}, u32[]{:S(2)}) collective-permute-start(bf16[1,2,24,576]{3,2,1,0:T(8,128)(2,1)S(1)} %get-tuple-element.598), channel_id=1, source_target_pairs={{0,1},{1,2},{2,3},{3,4},{4,5},{5,6},{6,7},{7,8},{8,9},{9,10},{10,1... | collective-permute-start | bytes 165896 | tf_op jit(solution)/shard_map/while/body/eval_jaxpr/ppermute | solution.py:22
  157.6 5.8 %collective-permute-start = (bf16[1,2,24,576]{3,2,1,0:T(8,128)(2,1)S(1)}, bf16[1,2,24,576]{3,2,1,0:T(8,128)(2,1)S(1)}, u32[]{:S(2)}, u32[]{:S(2)}) collective-permute-start(bf16[1,2,24,576]{3,2,1,0:T(8,128)(2,1)S(1)} %get-tuple-element.598), channel_id=1, source_target_pairs={{0,1},{1,2},{2,3},{3,4},{4,5},{5,6},{6,7},{7,8},{8,9},{9,10},{10,1... | collective-permute-start | bytes 165896 | tf_op jit(solution)/shard_map/while/body/eval_jaxpr/ppermute | solution.py:22
  173.6 5.8 %collective-permute-start = (bf16[1,2,24,576]{3,2,1,0:T(8,128)(2,1)S(1)}, bf16[1,2,24,576]{3,2,1,0:T(8,128)(2,1)S(1)}, u32[]{:S(2)}, u32[]{:S(2)}) collective-permute-start(bf16[1,2,24,576]{3,2,1,0:T(8,128)(2,1)S(1)} %get-tuple-element.598), channel_id=1, source_target_pairs={{0,1},{1,2},{2,3},{3,4},{4,5},{5,6},{6,7},{7,8},{8,9},{9,10},{10,1... | collective-permute-start | bytes 165896 | tf_op jit(solution)/shard_map/while/body/eval_jaxpr/ppermute | solution.py:22
  189.5 5.8 %collective-permute-start = (bf16[1,2,24,576]{3,2,1,0:T(8,128)(2,1)S(1)}, bf16[1,2,24,576]{3,2,1,0:T(8,128)(2,1)S(1)}, u32[]{:S(2)}, u32[]{:S(2)}) collective-permute-start(bf16[1,2,24,576]{3,2,1,0:T(8,128)(2,1)S(1)} %get-tuple-element.598), channel_id=1, source_target_pairs={{0,1},{1,2},{2,3},{3,4},{4,5},{5,6},{6,7},{7,8},{8,9},{9,10},{10,1... | collective-permute-start | bytes 165896 | tf_op jit(solution)/shard_map/while/body/eval_jaxpr/ppermute | solution.py:22
  205.5 5.8 %collective-permute-start = (bf16[1,2,24,576]{3,2,1,0:T(8,128)(2,1)S(1)}, bf16[1,2,24,576]{3,2,1,0:T(8,128)(2,1)S(1)}, u32[]{:S(2)}, u32[]{:S(2)}) collective-permute-start(bf16[1,2,24,576]{3,2,1,0:T(8,128)(2,1)S(1)} %get-tuple-element.598), channel_id=1, source_target_pairs={{0,1},{1,2},{2,3},{3,4},{4,5},{5,6},{6,7},{7,8},{8,9},{9,10},{10,1... | collective-permute-start | bytes 165896 | tf_op jit(solution)/shard_map/while/body/eval_jaxpr/ppermute | solution.py:22
  221.5 5.8 %collective-permute-start = (bf16[1,2,24,576]{3,2,1,0:T(8,128)(2,1)S(1)}, bf16[1,2,24,576]{3,2,1,0:T(8,128)(2,1)S(1)}, u32[]{:S(2)}, u32[]{:S(2)}) collective-permute-start(bf16[1,2,24,576]{3,2,1,0:T(8,128)(2,1)S(1)} %get-tuple-element.598), channel_id=1, source_target_pairs={{0,1},{1,2},{2,3},{3,4},{4,5},{5,6},{6,7},{7,8},{8,9},{9,10},{10,1... | collective-permute-start | bytes 165896 | tf_op jit(solution)/shard_map/while/body/eval_jaxpr/ppermute | solution.py:22
  237.5 5.8 %collective-permute-start = (bf16[1,2,24,576]{3,2,1,0:T(8,128)(2,1)S(1)}, bf16[1,2,24,576]{3,2,1,0:T(8,128)(2,1)S(1)}, u32[]{:S(2)}, u32[]{:S(2)}) collective-permute-start(bf16[1,2,24,576]{3,2,1,0:T(8,128)(2,1)S(1)} %get-tuple-element.598), channel_id=1, source_target_pairs={{0,1},{1,2},{2,3},{3,4},{4,5},{5,6},{6,7},{7,8},{8,9},{9,10},{10,1... | collective-permute-start | bytes 165896 | tf_op jit(solution)/shard_map/while/body/eval_jaxpr/ppermute | solution.py:22
  253.4 5.8 %collective-permute-start = (bf16[1,2,24,576]{3,2,1,0:T(8,128)(2,1)S(1)}, bf16[1,2,24,576]{3,2,1,0:T(8,128)(2,1)S(1)}, u32[]{:S(2)}, u32[]{:S(2)}) collective-permute-start(bf16[1,2,24,576]{3,2,1,0:T(8,128)(2,1)S(1)} %get-tuple-element.598), channel_id=1, source_target_pairs={{0,1},{1,2},{2,3},{3,4},{4,5},{5,6},{6,7},{7,8},{8,9},{9,10},{10,1... | collective-permute-start | bytes 165896 | tf_op jit(solution)/shard_map/while/body/eval_jaxpr/ppermute | solution.py:22
  269.4 5.8 %collective-permute-start = (bf16[1,2,24,576]{3,2,1,0:T(8,128)(2,1)S(1)}, bf16[1,2,24,576]{3,2,1,0:T(8,128)(2,1)S(1)}, u32[]{:S(2)}, u32[]{:S(2)}) collective-permute-start(bf16[1,2,24,576]{3,2,1,0:T(8,128)(2,1)S(1)} %get-tuple-element.598), channel_id=1, source_target_pairs={{0,1},{1,2},{2,3},{3,4},{4,5},{5,6},{6,7},{7,8},{8,9},{9,10},{10,1... | collective-permute-start | bytes 165896 | tf_op jit(solution)/shard_map/while/body/eval_jaxpr/ppermute | solution.py:22
  285.4 5.8 %collective-permute-start = (bf16[1,2,24,576]{3,2,1,0:T(8,128)(2,1)S(1)}, bf16[1,2,24,576]{3,2,1,0:T(8,128)(2,1)S(1)}, u32[]{:S(2)}, u32[]{:S(2)}) collective-permute-start(bf16[1,2,24,576]{3,2,1,0:T(8,128)(2,1)S(1)} %get-tuple-element.598), channel_id=1, source_target_pairs={{0,1},{1,2},{2,3},{3,4},{4,5},{5,6},{6,7},{7,8},{8,9},{9,10},{10,1... | collective-permute-start | bytes 165896 | tf_op jit(solution)/shard_map/while/body/eval_jaxpr/ppermute | solution.py:22
  301.3 5.8 %collective-permute-start = (bf16[1,2,24,576]{3,2,1,0:T(8,128)(2,1)S(1)}, bf16[1,2,24,576]{3,2,1,0:T(8,128)(2,1)S(1)}, u32[]{:S(2)}, u32[]{:S(2)}) collective-permute-start(bf16[1,2,24,576]{3,2,1,0:T(8,128)(2,1)S(1)} %get-tuple-element.598), channel_id=1, source_target_pairs={{0,1},{1,2},{2,3},{3,4},{4,5},{5,6},{6,7},{7,8},{8,9},{9,10},{10,1... | collective-permute-start | bytes 165896 | tf_op jit(solution)/shard_map/while/body/eval_jaxpr/ppermute | solution.py:22
  317.3 5.8 %collective-permute-start = (bf16[1,2,24,576]{3,2,1,0:T(8,128)(2,1)S(1)}, bf16[1,2,24,576]{3,2,1,0:T(8,128)(2,1)S(1)}, u32[]{:S(2)}, u32[]{:S(2)}) collective-permute-start(bf16[1,2,24,576]{3,2,1,0:T(8,128)(2,1)S(1)} %get-tuple-element.598), channel_id=1, source_target_pairs={{0,1},{1,2},{2,3},{3,4},{4,5},{5,6},{6,7},{7,8},{8,9},{9,10},{10,1... | collective-permute-start | bytes 165896 | tf_op jit(solution)/shard_map/while/body/eval_jaxpr/ppermute | solution.py:22
  333.3 5.8 %collective-permute-start = (bf16[1,2,24,576]{3,2,1,0:T(8,128)(2,1)S(1)}, bf16[1,2,24,576]{3,2,1,0:T(8,128)(2,1)S(1)}, u32[]{:S(2)}, u32[]{:S(2)}) collective-permute-start(bf16[1,2,24,576]{3,2,1,0:T(8,128)(2,1)S(1)} %get-tuple-element.598), channel_id=1, source_target_pairs={{0,1},{1,2},{2,3},{3,4},{4,5},{5,6},{6,7},{7,8},{8,9},{9,10},{10,1... | collective-permute-start | bytes 165896 | tf_op jit(solution)/shard_map/while/body/eval_jaxpr/ppermute | solution.py:22
  349.3 5.8 %collective-permute-start = (bf16[1,2,24,576]{3,2,1,0:T(8,128)(2,1)S(1)}, bf16[1,2,24,576]{3,2,1,0:T(8,128)(2,1)S(1)}, u32[]{:S(2)}, u32[]{:S(2)}) collective-permute-start(bf16[1,2,24,576]{3,2,1,0:T(8,128)(2,1)S(1)} %get-tuple-element.598), channel_id=1, source_target_pairs={{0,1},{1,2},{2,3},{3,4},{4,5},{5,6},{6,7},{7,8},{8,9},{9,10},{10,1... | collective-permute-start | bytes 165896 | tf_op jit(solution)/shard_map/while/body/eval_jaxpr/ppermute | solution.py:22
  365.2 5.8 %collective-permute-start = (bf16[1,2,24,576]{3,2,1,0:T(8,128)(2,1)S(1)}, bf16[1,2,24,576]{3,2,1,0:T(8,128)(2,1)S(1)}, u32[]{:S(2)}, u32[]{:S(2)}) collective-permute-start(bf16[1,2,24,576]{3,2,1,0:T(8,128)(2,1)S(1)} %get-tuple-element.598), channel_id=1, source_target_pairs={{0,1},{1,2},{2,3},{3,4},{4,5},{5,6},{6,7},{7,8},{8,9},{9,10},{10,1... | collective-permute-start | bytes 165896 | tf_op jit(solution)/shard_map/while/body/eval_jaxpr/ppermute | solution.py:22
  381.2 5.8 %collective-permute-start = (bf16[1,2,24,576]{3,2,1,0:T(8,128)(2,1)S(1)}, bf16[1,2,24,576]{3,2,1,0:T(8,128)(2,1)S(1)}, u32[]{:S(2)}, u32[]{:S(2)}) collective-permute-start(bf16[1,2,24,576]{3,2,1,0:T(8,128)(2,1)S(1)} %get-tuple-element.598), channel_id=1, source_target_pairs={{0,1},{1,2},{2,3},{3,4},{4,5},{5,6},{6,7},{7,8},{8,9},{9,10},{10,1... | collective-permute-start | bytes 165896 | tf_op jit(solution)/shard_map/while/body/eval_jaxpr/ppermute | solution.py:22
  397.2 5.8 %collective-permute-start = (bf16[1,2,24,576]{3,2,1,0:T(8,128)(2,1)S(1)}, bf16[1,2,24,576]{3,2,1,0:T(8,128)(2,1)S(1)}, u32[]{:S(2)}, u32[]{:S(2)}) collective-permute-start(bf16[1,2,24,576]{3,2,1,0:T(8,128)(2,1)S(1)} %get-tuple-element.598), channel_id=1, source_target_pairs={{0,1},{1,2},{2,3},{3,4},{4,5},{5,6},{6,7},{7,8},{8,9},{9,10},{10,1... | collective-permute-start | bytes 165896 | tf_op jit(solution)/shard_map/while/body/eval_jaxpr/ppermute | solution.py:22
  413.1 5.8 %collective-permute-start = (bf16[1,2,24,576]{3,2,1,0:T(8,128)(2,1)S(1)}, bf16[1,2,24,576]{3,2,1,0:T(8,128)(2,1)S(1)}, u32[]{:S(2)}, u32[]{:S(2)}) collective-permute-start(bf16[1,2,24,576]{3,2,1,0:T(8,128)(2,1)S(1)} %get-tuple-element.598), channel_id=1, source_target_pairs={{0,1},{1,2},{2,3},{3,4},{4,5},{5,6},{6,7},{7,8},{8,9},{9,10},{10,1... | collective-permute-start | bytes 165896 | tf_op jit(solution)/shard_map/while/body/eval_jaxpr/ppermute | solution.py:22
  429.1 5.8 %collective-permute-start = (bf16[1,2,24,576]{3,2,1,0:T(8,128)(2,1)S(1)}, bf16[1,2,24,576]{3,2,1,0:T(8,128)(2,1)S(1)}, u32[]{:S(2)}, u32[]{:S(2)}) collective-permute-start(bf16[1,2,24,576]{3,2,1,0:T(8,128)(2,1)S(1)} %get-tuple-element.598), channel_id=1, source_target_pairs={{0,1},{1,2},{2,3},{3,4},{4,5},{5,6},{6,7},{7,8},{8,9},{9,10},{10,1... | collective-permute-start | bytes 165896 | tf_op jit(solution)/shard_map/while/body/eval_jaxpr/ppermute | solution.py:22
  445.1 5.8 %collective-permute-start = (bf16[1,2,24,576]{3,2,1,0:T(8,128)(2,1)S(1)}, bf16[1,2,24,576]{3,2,1,0:T(8,128)(2,1)S(1)}, u32[]{:S(2)}, u32[]{:S(2)}) collective-permute-start(bf16[1,2,24,576]{3,2,1,0:T(8,128)(2,1)S(1)} %get-tuple-element.598), channel_id=1, source_target_pairs={{0,1},{1,2},{2,3},{3,4},{4,5},{5,6},{6,7},{7,8},{8,9},{9,10},{10,1... | collective-permute-start | bytes 165896 | tf_op jit(solution)/shard_map/while/body/eval_jaxpr/ppermute | solution.py:22
  461.0 5.8 %collective-permute-start = (bf16[1,2,24,576]{3,2,1,0:T(8,128)(2,1)S(1)}, bf16[1,2,24,576]{3,2,1,0:T(8,128)(2,1)S(1)}, u32[]{:S(2)}, u32[]{:S(2)}) collective-permute-start(bf16[1,2,24,576]{3,2,1,0:T(8,128)(2,1)S(1)} %get-tuple-element.598), channel_id=1, source_target_pairs={{0,1},{1,2},{2,3},{3,4},{4,5},{5,6},{6,7},{7,8},{8,9},{9,10},{10,1... | collective-permute-start | bytes 165896 | tf_op jit(solution)/shard_map/while/body/eval_jaxpr/ppermute | solution.py:22
  477.0 5.8 %collective-permute-start = (bf16[1,2,24,576]{3,2,1,0:T(8,128)(2,1)S(1)}, bf16[1,2,24,576]{3,2,1,0:T(8,128)(2,1)S(1)}, u32[]{:S(2)}, u32[]{:S(2)}) collective-permute-start(bf16[1,2,24,576]{3,2,1,0:T(8,128)(2,1)S(1)} %get-tuple-element.598), channel_id=1, source_target_pairs={{0,1},{1,2},{2,3},{3,4},{4,5},{5,6},{6,7},{7,8},{8,9},{9,10},{10,1... | collective-permute-start | bytes 165896 | tf_op jit(solution)/shard_map/while/body/eval_jaxpr/ppermute | solution.py:22
  493.0 5.8 %collective-permute-start = (bf16[1,2,24,576]{3,2,1,0:T(8,128)(2,1)S(1)}, bf16[1,2,24,576]{3,2,1,0:T(8,128)(2,1)S(1)}, u32[]{:S(2)}, u32[]{:S(2)}) collective-permute-start(bf16[1,2,24,576]{3,2,1,0:T(8,128)(2,1)S(1)} %get-tuple-element.598), channel_id=1, source_target_pairs={{0,1},{1,2},{2,3},{3,4},{4,5},{5,6},{6,7},{7,8},{8,9},{9,10},{10,1... | collective-permute-start | bytes 165896 | tf_op jit(solution)/shard_map/while/body/eval_jaxpr/ppermute | solution.py:22
  509.0 5.8 %collective-permute-start = (bf16[1,2,24,576]{3,2,1,0:T(8,128)(2,1)S(1)}, bf16[1,2,24,576]{3,2,1,0:T(8,128)(2,1)S(1)}, u32[]{:S(2)}, u32[]{:S(2)}) collective-permute-start(bf16[1,2,24,576]{3,2,1,0:T(8,128)(2,1)S(1)} %get-tuple-element.598), channel_id=1, source_target_pairs={{0,1},{1,2},{2,3},{3,4},{4,5},{5,6},{6,7},{7,8},{8,9},{9,10},{10,1... | collective-permute-start | bytes 165896 | tf_op jit(solution)/shard_map/while/body/eval_jaxpr/ppermute | solution.py:22
  (3 other events, 5.0 us)
